TPU v7x, 32 devices: a whole 2x2x4 slice. The times are simulated.
32 devices in a mesh: ctx: 8 (over z, x), fsdp: 4 (over y, core).
Axes of the slice: x: 2, y: 2, z: 4, core: 2. Of those that a mesh axis runs over, the one named last changes fastest.
Arguments:
- tokens: bfloat16 [4, 1024, 1536], P('fsdp', 'ctx'), may hold values from -6 to 6
- segments: int32 [4, 1024], P('fsdp'), may hold values from 0 to 3, never falling along the last dimension, each value on 1 to 512 neighbouring positions
- gain_attn: bfloat16 [1536], replicated, may hold values from 0.5 to 1.5
- w_query: bfloat16 [1536, 1536], P('fsdp'), may hold values from -0.15625 to 0.15625
- w_key: bfloat16 [1536, 1536], P('fsdp'), may hold values from -0.15625 to 0.15625
- w_value: bfloat16 [1536, 1536], P('fsdp'), may hold values from -0.15625 to 0.15625
- w_forget: bfloat16 [1536, 24], P('fsdp'), may hold values from -0.15625 to 0.15625
- forget_bias: float32 [24], replicated, may hold values from 2 to 8
- w_outgate: bfloat16 [1536, 1536], P('fsdp'), may hold values from -0.15625 to 0.15625
- w_out: bfloat16 [1536, 1536], P('fsdp'), may hold values from -0.625 to 0.625
- gain_ffn: bfloat16 [1536], replicated, may hold values from 0.5 to 1.5
- w_gate: bfloat16 [1536, 4096], P('fsdp'), may hold values from -0.15625 to 0.15625
- w_up: bfloat16 [1536, 4096], P('fsdp'), may hold values from -0.15625 to 0.15625
- w_down: bfloat16 [4096, 1536], P('fsdp'), may hold values from -0.09375 to 0.09375
- cotangent: bfloat16 [4, 1024, 1536], P('fsdp', 'ctx'), may hold values from -6 to 6
Outputs:
- output: bfloat16 [4, 1024, 1536], P('fsdp', 'ctx')
- grad_tokens: float32 [4, 1024, 1536], P('fsdp', 'ctx')
- grad_gain_attn: float32 [1536], replicated
- grad_query: float32 [1536, 1536], P('fsdp')
- grad_key: float32 [1536, 1536], P('fsdp')
- grad_value: float32 [1536, 1536], P('fsdp')
- grad_forget: float32 [1536, 24], P('fsdp')
- grad_bias: float32 [24], replicated
- grad_outgate: float32 [1536, 1536], P('fsdp')
- grad_out: float32 [1536, 1536], P('fsdp')
- grad_gain_ffn: float32 [1536], replicated
- grad_gate: float32 [1536, 4096], P('fsdp')
- grad_up: float32 [1536, 4096], P('fsdp')
- grad_down: float32 [4096, 1536], P('fsdp')
Inputs may be any that keep to these rules, and one draw needn't show every extreme that they name: `segments`: along each sequence the document numbers never fall; every document has 1 to 512 tokens and one has exactly 512.
All inputs are finite; a program needn't handle non-finite values.
Results may differ from a plain program's by a relative error of at most 0.014.
Values may be sent and summed in bfloat16 or wider, within the bound.
A program may use at most 448 MiB of HBM per device.

v0:
```python
import math
import jax
import jax.numpy as jnp
from jax import lax
from jax.sharding import PartitionSpec as P

EPSILON = 1e-06
NEGATIVE = -1e30


def entering(value, axis, join, neutral, backward):
    count, mine = (lax.axis_size(axis), lax.axis_index(axis))
    pieces = lax.all_gather(value, axis)
    if backward:
        pieces = pieces[::-1]
        mine = count - 1 - mine
    subtotal = jnp.full_like(value, 0) + jnp.asarray(neutral, value.dtype)

    def hop(position, subtotal):
        longer = join(subtotal, pieces[position])
        return jnp.where(position < mine, longer, subtotal)

    return lax.fori_loop(0, count - 1, hop, subtotal)


def matmul(left, right):
    return jnp.dot(left, right, preferred_element_type=jnp.float32)


def matmul_rows(left, right):
    return lax.dot_general(
        left, right, (((1,), (1,)), ((), ())), preferred_element_type=jnp.float32
    )


def weight_grad(left, right):
    return lax.dot_general(
        left, right, (((0,), (0,)), ((), ())), preferred_element_type=jnp.float32
    )


def rms_stats(values):
    rstat = lax.rsqrt(jnp.mean(values * values, axis=-1, keepdims=True) + EPSILON)
    return (values * rstat, rstat)


def norm_back(grad_in, normed, rstat, gain):
    grad_normed = grad_in * gain
    grad_gain = jnp.sum(grad_in * normed, axis=0)
    grad_values = rstat * (
        grad_normed - normed * jnp.mean(grad_normed * normed, axis=-1, keepdims=True)
    )
    return (grad_values, grad_gain)


def shards(
    tokens,
    segments,
    gain_attn,
    w_query,
    w_key,
    w_value,
    w_forget,
    forget_bias,
    w_outgate,
    w_out,
    gain_ffn,
    w_gate,
    w_up,
    w_down,
    cotangent,
):
    gathered = (
        lax.all_gather(w_query, "fsdp", axis=0, tiled=True),
        lax.all_gather(w_key, "fsdp", axis=0, tiled=True),
        lax.all_gather(w_value, "fsdp", axis=0, tiled=True),
        lax.all_gather(w_forget, "fsdp", axis=0, tiled=True),
        lax.all_gather(w_outgate, "fsdp", axis=0, tiled=True),
        lax.all_gather(w_out, "fsdp", axis=0, tiled=True),
        lax.all_gather(w_gate, "fsdp", axis=0, tiled=True),
        lax.all_gather(w_up, "fsdp", axis=0, tiled=True),
        lax.all_gather(w_down, "fsdp", axis=0, tiled=True),
    )
    (
        full_query,
        full_key,
        full_value,
        full_forget,
        full_outgate,
        full_out,
        full_gate,
        full_up,
        full_down,
    ) = gathered
    inputs = tokens[0].astype(jnp.float32)
    tok_rows = inputs.shape[0]
    model_width = inputs.shape[1]
    n_heads = forget_bias.shape[0]
    head_dim = model_width // n_heads
    per_group = math.gcd(n_heads, 2)
    n_groups = n_heads // per_group
    group_width = per_group * head_dim
    scaling = head_dim ** (-0.5)
    n_ctx = lax.axis_size("ctx")
    position = lax.axis_index("ctx")
    seq_rows = tok_rows * n_ctx
    seg_all = segments[0]
    first_row = position * tok_rows
    pos_here = first_row + jnp.arange(tok_rows, dtype=jnp.int32)
    seg_here = lax.dynamic_slice_in_dim(seg_all, first_row, tok_rows, 0)
    pos_all = jnp.arange(seq_rows, dtype=jnp.int32)
    allowed = (pos_all[None, :] <= pos_here[:, None]) & (seg_all[None, :] == seg_here[:, None])
    gain_one = gain_attn.astype(jnp.float32)
    normed_one, rstat_one = rms_stats(inputs)
    normed = (normed_one * gain_one).astype(jnp.bfloat16)
    queries = matmul(normed, full_query).astype(jnp.bfloat16)
    key_own = matmul(normed, full_key).astype(jnp.bfloat16)
    value_own = matmul(normed, full_value).astype(jnp.bfloat16)
    forget_logits = matmul(normed, full_forget) + forget_bias
    log_keep = jax.nn.log_sigmoid(forget_logits)
    before = entering(
        jnp.sum(log_keep, axis=0), "ctx", jnp.add, jnp.zeros((n_heads,), jnp.float32), False
    )
    sent_rows = before[None, :] + jnp.cumsum(log_keep, axis=0)
    arrived = lax.all_gather(sent_rows, "ctx", axis=0, tiled=True)
    keys_all, values_all = (
        lax.all_gather(key_own, "ctx", axis=0, tiled=True),
        lax.all_gather(value_own, "ctx", axis=0, tiled=True),
    )

    def group_slices(group_index):
        column = group_index * group_width
        query_part = lax.dynamic_slice_in_dim(queries, column, group_width, 1).reshape(
            tok_rows, per_group, head_dim
        )
        key_part = lax.dynamic_slice_in_dim(keys_all, column, group_width, 1).reshape(
            seq_rows, per_group, head_dim
        )
        value_part = lax.dynamic_slice_in_dim(values_all, column, group_width, 1).reshape(
            seq_rows, per_group, head_dim
        )
        decay_rows = lax.dynamic_slice_in_dim(sent_rows, group_index * per_group, per_group, 1)
        decay_keys = lax.dynamic_slice_in_dim(arrived, group_index * per_group, per_group, 1)
        scores = (
            jnp.einsum("bhd,nhd->hbn", query_part, key_part, preferred_element_type=jnp.float32)
            * scaling
        )
        scores = scores + decay_rows.T[:, :, None] - decay_keys.T[:, None, :]
        scores = jnp.where(allowed[None], scores, NEGATIVE)
        return (query_part, key_part, value_part, scores)

    def forward_group(group_index):
        query_part, key_part, value_part, scores = group_slices(group_index)
        row_max = jnp.max(scores, axis=-1, keepdims=True)
        raised = jnp.exp(scores - row_max)
        row_total = jnp.sum(raised, axis=-1, keepdims=True)
        probabilities = raised / row_total
        mixed_part = jnp.einsum(
            "hbn,nhd->bhd",
            probabilities.astype(jnp.bfloat16),
            value_part,
            preferred_element_type=jnp.float32,
        )
        return (mixed_part.reshape(tok_rows, group_width), (row_max + jnp.log(row_total))[:, :, 0])

    mixed_groups, log_totals = lax.map(forward_group, jnp.arange(n_groups, dtype=jnp.int32))
    attended = jnp.moveaxis(mixed_groups, 0, 1).reshape(tok_rows, model_width)
    gate_logits = matmul(normed, full_outgate)
    gate_value = jax.nn.sigmoid(gate_logits)
    gated_out = (attended * gate_value).astype(jnp.bfloat16)
    middle = inputs + matmul(gated_out, full_out)
    gain_two = gain_ffn.astype(jnp.float32)
    normed_two_f, rstat_two = rms_stats(middle)
    normed_two = (normed_two_f * gain_two).astype(jnp.bfloat16)
    gate_part = matmul(normed_two, full_gate)
    up_part = matmul(normed_two, full_up)
    sig_gate = jax.nn.sigmoid(gate_part)
    silu_gate = gate_part * sig_gate
    hidden = (silu_gate * up_part).astype(jnp.bfloat16)
    output = middle + matmul(hidden, full_down)
    grad_out_low = cotangent[0]
    grad_output = grad_out_low.astype(jnp.float32)
    grad_hidden = matmul_rows(grad_out_low, full_down)
    grad_gate_low = (
        grad_hidden * up_part * (sig_gate * (1.0 + gate_part * (1.0 - sig_gate)))
    ).astype(jnp.bfloat16)
    grad_up_low = (grad_hidden * silu_gate).astype(jnp.bfloat16)
    grad_normed_two = matmul_rows(grad_gate_low, full_gate) + matmul_rows(grad_up_low, full_up)
    back_two, grad_gain_two = norm_back(grad_normed_two, normed_two_f, rstat_two, gain_two)
    grad_middle = grad_output + back_two
    ffn_parts = (
        lax.psum_scatter(
            weight_grad(normed_two, grad_gate_low), "fsdp", scatter_dimension=0, tiled=True
        ),
        lax.psum_scatter(
            weight_grad(normed_two, grad_up_low), "fsdp", scatter_dimension=0, tiled=True
        ),
        lax.psum_scatter(
            weight_grad(hidden, grad_out_low), "fsdp", scatter_dimension=0, tiled=True
        ),
    )
    grad_branch_low = grad_middle.astype(jnp.bfloat16)
    grad_gated = matmul_rows(grad_branch_low, full_out)
    grad_attn_low = (grad_gated * gate_value).astype(jnp.bfloat16)
    grad_gatelog_low = (grad_gated * attended * (gate_value * (1.0 - gate_value))).astype(
        jnp.bfloat16
    )

    def backward_group(group_index, carried):
        grad_queries, grad_keys, grad_values, grad_rowdecay, grad_keydecay = carried
        query_part, key_part, value_part, scores = group_slices(group_index)
        probabilities = jnp.exp(scores - log_totals[group_index][:, :, None])
        column = group_index * group_width
        grad_part = lax.dynamic_slice_in_dim(grad_attn_low, column, group_width, 1).reshape(
            tok_rows, per_group, head_dim
        )
        grad_vpart = jnp.einsum(
            "hbn,bhd->nhd",
            probabilities.astype(jnp.bfloat16),
            grad_part,
            preferred_element_type=jnp.float32,
        )
        grad_probs = jnp.einsum(
            "bhd,nhd->hbn", grad_part, value_part, preferred_element_type=jnp.float32
        )
        row_inner = jnp.sum(probabilities * grad_probs, axis=-1, keepdims=True)
        grad_scores = (probabilities * (grad_probs - row_inner)).astype(jnp.bfloat16)
        grad_qpart = (
            jnp.einsum("hbn,nhd->bhd", grad_scores, key_part, preferred_element_type=jnp.float32)
            * scaling
        )
        grad_kpart = (
            jnp.einsum("hbn,bhd->nhd", grad_scores, query_part, preferred_element_type=jnp.float32)
            * scaling
        )
        score_sums = grad_scores.astype(jnp.float32)
        grad_queries = lax.dynamic_update_slice_in_dim(
            grad_queries, grad_qpart.reshape(tok_rows, group_width), column, 1
        )
        grad_keys = lax.dynamic_update_slice_in_dim(
            grad_keys, grad_kpart.reshape(seq_rows, group_width), column, 1
        )
        grad_values = lax.dynamic_update_slice_in_dim(
            grad_values, grad_vpart.reshape(seq_rows, group_width), column, 1
        )
        grad_rowdecay = lax.dynamic_update_slice_in_dim(
            grad_rowdecay, jnp.sum(score_sums, axis=-1).T, group_index * per_group, 1
        )
        grad_keydecay = lax.dynamic_update_slice_in_dim(
            grad_keydecay, -jnp.sum(score_sums, axis=1).T, group_index * per_group, 1
        )
        return (grad_queries, grad_keys, grad_values, grad_rowdecay, grad_keydecay)

    initial = (
        jnp.zeros((tok_rows, model_width), jnp.float32),
        jnp.zeros((seq_rows, model_width), jnp.float32),
        jnp.zeros((seq_rows, model_width), jnp.float32),
        jnp.zeros((tok_rows, n_heads), jnp.float32),
        jnp.zeros((seq_rows, n_heads), jnp.float32),
    )
    grad_queries, grad_keys, grad_values, grad_rowdecay, grad_keydecay = lax.fori_loop(
        0, n_groups, backward_group, initial
    )
    key_back = (
        lax.psum_scatter(grad_keys, "ctx", scatter_dimension=0, tiled=True),
        lax.psum_scatter(grad_values, "ctx", scatter_dimension=0, tiled=True),
        lax.psum_scatter(grad_keydecay, "ctx", scatter_dimension=0, tiled=True),
    )
    grad_query_low = grad_queries.astype(jnp.bfloat16)
    grad_key_low = key_back[0].astype(jnp.bfloat16)
    grad_value_low = key_back[1].astype(jnp.bfloat16)
    decay_grad = grad_rowdecay + key_back[2]
    local_suffix = jnp.flip(jnp.cumsum(jnp.flip(decay_grad, 0), axis=0), 0)
    block_total = jnp.sum(decay_grad, axis=0)
    later_sum = entering(block_total, "ctx", jnp.add, jnp.zeros((n_heads,), jnp.float32), True)
    grad_logits_low = ((local_suffix + later_sum[None, :]) * jax.nn.sigmoid(-forget_logits)).astype(
        jnp.bfloat16
    )
    grad_bias = jnp.sum(grad_logits_low.astype(jnp.float32), axis=0)
    grad_normed = (
        matmul_rows(grad_query_low, full_query)
        + matmul_rows(grad_key_low, full_key)
        + matmul_rows(grad_value_low, full_value)
        + matmul_rows(grad_logits_low, full_forget)
        + matmul_rows(grad_gatelog_low, full_outgate)
    )
    back_one, grad_gain_one = norm_back(grad_normed, normed_one, rstat_one, gain_one)
    grad_inputs = grad_middle + back_one
    attn_parts = (
        lax.psum_scatter(
            weight_grad(normed, grad_query_low), "fsdp", scatter_dimension=0, tiled=True
        ),
        lax.psum_scatter(
            weight_grad(normed, grad_key_low), "fsdp", scatter_dimension=0, tiled=True
        ),
        lax.psum_scatter(
            weight_grad(normed, grad_value_low), "fsdp", scatter_dimension=0, tiled=True
        ),
        lax.psum_scatter(
            weight_grad(normed, grad_logits_low), "fsdp", scatter_dimension=0, tiled=True
        ),
        lax.psum_scatter(
            weight_grad(normed, grad_gatelog_low), "fsdp", scatter_dimension=0, tiled=True
        ),
        lax.psum_scatter(
            weight_grad(gated_out, grad_branch_low), "fsdp", scatter_dimension=0, tiled=True
        ),
    )
    summed = lax.psum(
        (
            ffn_parts[0],
            ffn_parts[1],
            ffn_parts[2],
            attn_parts[0],
            attn_parts[1],
            attn_parts[2],
            attn_parts[3],
            attn_parts[4],
            attn_parts[5],
        ),
        "ctx",
    )
    small_grads = lax.psum((grad_gain_one, grad_gain_two, grad_bias), ("ctx", "fsdp"))
    return (
        output.astype(jnp.bfloat16)[None],
        grad_inputs[None],
        small_grads[0],
        summed[3],
        summed[4],
        summed[5],
        summed[6],
        small_grads[2],
        summed[7],
        summed[8],
        small_grads[1],
        summed[0],
        summed[1],
        summed[2],
    )


def solution(mesh):
    return jax.shard_map(
        shards,
        mesh=mesh,
        in_specs=(
            P("fsdp", "ctx", None),
            P("fsdp", None),
            P(),
            P("fsdp", None),
            P("fsdp", None),
            P("fsdp", None),
            P("fsdp", None),
            P(),
            P("fsdp", None),
            P("fsdp", None),
            P(),
            P("fsdp", None),
            P("fsdp", None),
            P("fsdp", None),
            P("fsdp", "ctx", None),
        ),
        out_specs=(
            P("fsdp", "ctx", None),
            P("fsdp", "ctx", None),
            P(),
            P("fsdp", None),
            P("fsdp", None),
            P("fsdp", None),
            P("fsdp", None),
            P(),
            P("fsdp", None),
            P("fsdp", None),
            P(),
            P("fsdp", None),
            P("fsdp", None),
            P("fsdp", None),
        ),
        check_vma=False,
    )
```

profile of v0, /device:TPU:0, one launch (start us, length us, event | category | flops | bytes accessed | tf_op | source)
XLA Modules:
  0.0 2965.8 jit_solution(18028929066030934375)
XLA Ops:
  11.3 38.5 %all-gather.13.cloned.1.call-done = bf16[1536,1536]{1,0:T(8,128)(2,1)} async-done(((bf16[384,1536]{1,0:T(8,128)(2,1)}), bf16[1536,1536]{1,0:T(8,128)(2,1)}) %all-gather.13.cloned.1.call-update) | async-done | bytes 4718608 | tf_op jit(solution)/shard_map/all_gather | solution.py:76
  49.8 4.0 convolution_convert_fusion.2
  53.9 34.9 %all-gather.19.cloned.1.call-done = bf16[1536,1536]{1,0:T(8,128)(2,1)} async-done(((bf16[384,1536]{1,0:T(8,128)(2,1)}), bf16[1536,1536]{1,0:T(8,128)(2,1)}) %all-gather.19.cloned.1.call-update) | async-done | bytes 4718608 | tf_op jit(solution)/shard_map/all_gather | solution.py:75
  88.8 3.9 convolution_convert_fusion
  96.3 5.3 all_gather.51
  104.7 21.3 all-reduce
  127.3 32.3 %all_gather.53 = f32[1024,24]{1,0:T(8,128)S(1)} all-gather(f32[128,24]{1,0:T(8,128)S(1)} %broadcast_add_fusion), channel_id=1, replica_groups=mesh['ctx'=8,'fsdp'=4] {'ctx'}, dimensions={0}, use_global_device_ids=true | all-gather | bytes 110592 | tf_op jit(solution)/shard_map/all_gather | solution.py:125
  162.1 3.2 convolution_convert_fusion.1
  166.2 26.5 all-gather.15.cloned.1.call-done
  192.7 3.2 copy.45
  195.9 58.5 %all-gather.21.cloned.1.call-done = bf16[1024,1536]{1,0:T(8,128)(2,1)} async-done(((bf16[128,1536]{1,0:T(8,128)(2,1)}), bf16[1024,1536]{1,0:T(8,128)(2,1)}) %all-gather.21.cloned.1.call-update) | async-done | bytes 3145744 | tf_op jit(solution)/shard_map/all_gather | solution.py:127
  254.4 4.6 copy.47
  259.6 142.4 %while.63 = (s32[]{:T(128)}, f32[12,128,128]{1,2,0:T(8,128)}, f32[12,2,128]{2,1,0:T(2,128)}, s32[12]{0:T(128)}, bf16[1024,1536]{0,1:T(8,128)(2,1)S(1)}, /*index=...) while((s32[]{:T(128)}, f32[12,128,128]{1,2,0:T(8,128)}, ...), condition=%wide.region_8.9_spmd.clone, body=%wide.region_5.8_spmd.clone.sunk | while | flops 70123272 | bytes 5316909 | solution.py:166
  261.5 1.8 constant_dynamic-slice_fusion.16
  320.6 1.8 constant_dynamic-slice_fusion.16
  344.3 1.8 constant_dynamic-slice_fusion.16
  379.8 1.8 constant_dynamic-slice_fusion.16
  402.0 2.9 copy.50
  404.9 4.7 multiply_convert_fusion.6
  409.5 3.4 multiply_reduce_fusion.3
  414.8 7.7 fusion.77
  422.5 76.0 %all-gather.29.cloned.1.call-done = bf16[1536,4096]{1,0:T(8,128)(2,1)} async-done(((bf16[384,4096]{1,0:T(8,128)(2,1)}), bf16[1536,4096]{1,0:T(8,128)(2,1)}) %all-gather.29.cloned.1.call-update) | async-done | bytes 12582928 | tf_op jit(solution)/shard_map/all_gather | solution.py:81
  498.5 7.7 fusion.78
  506.2 75.9 %all-gather.31.cloned.1.call-done = bf16[4096,1536]{1,0:T(8,128)(2,1)} async-done(((bf16[1024,1536]{1,0:T(8,128)(2,1)}), bf16[4096,1536]{1,0:T(8,128)(2,1)}) %all-gather.31.cloned.1.call-update) | async-done | bytes 12582928 | tf_op jit(solution)/shard_map/all_gather | solution.py:82
  582.1 11.7 multiply_convert_fusion.1
  593.8 10.2 fusion.79
  604.0 7.4 multiply_reduce_fusion.1
  612.8 5.5 multiply_convert_fusion.4
  619.1 3.5 broadcast.106
  622.6 3.5 broadcast.106.clone
  626.1 118.0 %while.64 = (s32[]{:T(128)}, bf16[128,1536]{0,1:T(8,128)(2,1)}, f32[1024,1536]{0,1:T(8,128)}, f32[1024,1536]{0,1:T(8,128)}, f32[128,24]{0,1:T(8,128)S(1)}, /*ind...) while((s32[]{:T(128)}, bf16[128,1536]{0,1:T(8,128)(2,1)}, ...), condition=%wide.region_15.16_spmd.clone, body=%wide.region_11.15_spmd.clone.sunk | while | flops 171998720 | bytes 13599061 | solution.py:261
  745.6 5.2 fusion.52
  750.8 5.0 fusion.62
  757.0 6.0 fusion.56
  763.0 99.6 %reduce-scatter.13.cloned.1.call-done = f32[128,1536]{0,1:T(8,128)} async-done(((f32[1024,1536]{0,1:T(8,128)}), f32[128,1536]{0,1:T(8,128)}) %reduce-scatter.13.cloned.1.call-update) | async-done | bytes 786448 | tf_op jit(solution)/shard_map/reduce_scatter | solution.py:265
  862.6 6.2 fusion.49
  869.1 115.0 %reduce-scatter.15.cloned.1.call-done = f32[128,1536]{0,1:T(8,128)} async-done(((f32[1024,1536]{0,1:T(8,128)}), f32[128,1536]{0,1:T(8,128)}) %reduce-scatter.15.cloned.1.call-update) | async-done | bytes 786448 | tf_op jit(solution)/shard_map/reduce_scatter | solution.py:266
  984.2 6.2 fusion.46
  990.4 11.4 fusion.81
  1001.9 11.4 fusion.82
  1014.2 11.5 fusion.42
  1025.8 19.3 reduce-scatter.17.cloned.1.call-done
  1046.7 19.5 all-reduce.1
  1067.8 57.4 %reduce-scatter.19.cloned.1.call-done = f32[384,1536]{1,0:T(8,128)} async-done(((f32[1536,1536]{1,0:T(8,128)}), f32[384,1536]{1,0:T(8,128)}) %reduce-scatter.19.cloned.1.call-update) | async-done | bytes 2359312 | tf_op jit(solution)/shard_map/reduce_scatter | solution.py:290
  1125.1 80.9 %reduce-scatter.27.cloned.1.call-done = f32[384,1536]{1,0:T(8,128)} async-done(((f32[1536,1536]{1,0:T(8,128)}), f32[384,1536]{1,0:T(8,128)}) %reduce-scatter.27.cloned.1.call-update) | async-done | bytes 2359312 | tf_op jit(solution)/shard_map/reduce_scatter | solution.py:302
  1206.0 80.9 %reduce-scatter.29.cloned.1.call-done = f32[384,1536]{1,0:T(8,128)} async-done(((f32[1536,1536]{1,0:T(8,128)}), f32[384,1536]{1,0:T(8,128)}) %reduce-scatter.29.cloned.1.call-update) | async-done | bytes 2359312 | tf_op jit(solution)/shard_map/reduce_scatter | solution.py:305
  1286.9 80.9 %reduce-scatter.21.cloned.1.call-done = f32[384,1536]{1,0:T(8,128)} async-done(((f32[1536,1536]{1,0:T(8,128)}), f32[384,1536]{1,0:T(8,128)}) %reduce-scatter.21.cloned.1.call-update) | async-done | bytes 2359312 | tf_op jit(solution)/shard_map/reduce_scatter | solution.py:293
  1367.8 80.9 %reduce-scatter.23.cloned.1.call-done = f32[384,1536]{1,0:T(8,128)} async-done(((f32[1536,1536]{1,0:T(8,128)}), f32[384,1536]{1,0:T(8,128)}) %reduce-scatter.23.cloned.1.call-update) | async-done | bytes 2359312 | tf_op jit(solution)/shard_map/reduce_scatter | solution.py:296
  1448.8 183.1 %reduce-scatter.31.cloned.1.call-done = f32[384,4096]{1,0:T(8,128)} async-done(((f32[1536,4096]{1,0:T(8,128)}), f32[384,4096]{1,0:T(8,128)}) %reduce-scatter.31.cloned.1.call-update) | async-done | bytes 6291472 | tf_op jit(solution)/shard_map/reduce_scatter | solution.py:192
  1631.8 183.1 %reduce-scatter.33.cloned.1.call-done = f32[384,4096]{1,0:T(8,128)} async-done(((f32[1536,4096]{1,0:T(8,128)}), f32[384,4096]{1,0:T(8,128)}) %reduce-scatter.33.cloned.1.call-update) | async-done | bytes 6291472 | tf_op jit(solution)/shard_map/reduce_scatter | solution.py:195
  1814.9 183.1 %reduce-scatter.35.cloned.1.call-done = f32[1024,1536]{1,0:T(8,128)} async-done(((f32[4096,1536]{1,0:T(8,128)}), f32[1024,1536]{1,0:T(8,128)}) %reduce-scatter.35.cloned.1.call-update) | async-done | bytes 6291472 | tf_op jit(solution)/shard_map/reduce_scatter | solution.py:198
  1998.0 4.9 fusion.80
  2002.9 4.9 fusion.83
  2007.8 7.2 fusion.26
  2015.1 5.7 reduce-scatter.25.cloned.1.call-done
  2020.8 40.7 %psum.88 = f32[384,24]{0,1:T(8,128)} all-reduce(f32[384,24]{0,1:T(8,128)} %reduce-scatter.25.cloned.1.call-done), channel_id=1, replica_groups=mesh['ctx'=8,'fsdp'=4] {'ctx'}, use_global_device_ids=true, to_apply=%region_33.34 | all-reduce | flops 9216 | bytes 73728 | tf_op jit(solution)/shard_map/psum | solution.py:309
  2061.5 4.3 convolution_add_fusion.2
  2065.8 4.2 convolution_add_fusion.1
  2070.5 42.8 %all-reduce.2 = (f32[1536]{0:T(1024)}, f32[24]{0:T(128)}, f32[1536]{0:T(1024)}) all-reduce(f32[1536]{0:T(1024)S(1)} %get-tuple-element.623, f32[24]{0:T(128)S(1)} %get-tuple-element.709, f32[1536]{0:T(1024)S(1)} %copy-done.23), channel_id=1, replica_groups=mesh['ctx'=8,'fsdp'=4] {'ctx','fsdp'}, use_global_device_ids=true, to_apply=%region_25.26 | all-reduce | flops 3096 | bytes 24768 | tf_op jit(solution)/shard_map/psum | solution.py:323
  2114.5 822.6 %all-reduce.6.cloned.1.call-done = (f32[384,1536]{1,0:T(8,128)}, f32[384,1536]{1,0:T(8,128)}, f32[384,1536]{1,0:T(8,128)}, f32[384,1536]{1,0:T(8,128)}, f32[384,...) async-done(((f32[384,1536]{1,0:T(8,128)}, f32[384,1536]{1,0:T(8,128)}, f32[384,1536]{1,0:T(8,128)}, f32[384,1536]{1,0:T(8,128)}, ...) | async-done | bytes 30670864 | tf_op jit(solution)/shard_map/psum | solution.py:309
  2937.1 3.4 copy.121
  2948.2 3.2 copy.126
  2951.8 3.2 copy.127
  2956.3 2.7 copy.128
  (543 shorter events, 273.4 us)
Async XLA Ops:
  7.2 81.7 %copy-start.1 = (bf16[1,128,1536]{2,1,0:T(8,128)(2,1)S(1)}, bf16[1,128,1536]{2,1,0:T(8,128)(2,1)}, u32[]{:S(2)}) copy-start(bf16[1,128,1536]{2,1,0:T(8,128)(2,1)} %param.23) | copy-start | bytes 1179652
  7.2 42.6 %all-gather.13.cloned.1.call-start = ((), (), s32[]{:S(2)}) async-start(), calls=%async_computation.12 | async-start | bytes 5898240 | tf_op jit(solution)/shard_map/all_gather | solution.py:76
  7.9 80.9 %all-gather.19.cloned.1.call-start = ((), (), s32[]{:S(2)}) async-start(), calls=%async_computation.15 | async-start | bytes 5898240 | tf_op jit(solution)/shard_map/all_gather | solution.py:75
  8.7 153.4 %all-gather.17.cloned.1.call-start = ((), (), s32[]{:S(2)}) async-start(), calls=%async_computation.14 | async-start | bytes 5898240 | tf_op jit(solution)/shard_map/all_gather | solution.py:74
  9.4 183.3 %all-gather.15.cloned.1.call-start = ((), (), s32[]{:S(2)}) async-start(), calls=%async_computation.13 | async-start | bytes 3538944 | tf_op jit(solution)/shard_map/all_gather | solution.py:128
  53.9 200.6 %all-gather.21.cloned.1.call-start = ((), (), s32[]{:S(2)}) async-start(), calls=%async_computation.16 | async-start | bytes 3538944 | tf_op jit(solution)/shard_map/all_gather | solution.py:127
  92.8 312.1 %all-gather.23.cloned.1.call-start = ((), (), s32[]{:S(2)}) async-start(), calls=%async_computation.17 | async-start | bytes 5898240 | tf_op jit(solution)/shard_map/all_gather | solution.py:78
  93.4 316.2 %all-gather.25.cloned.1.call-start = ((), (), s32[]{:S(2)}) async-start(), calls=%async_computation.18 | async-start | bytes 5898240 | tf_op jit(solution)/shard_map/all_gather | solution.py:79
  94.1 2.2 copy-start.24
  94.1 8.1 copy-start.27
  94.1 9.2 copy-start.28
  94.1 320.6 %all-gather.27.cloned.1.call-start = ((), (), s32[]{:S(2)}) async-start(), calls=%async_computation.19 | async-start | bytes 15728640 | tf_op jit(solution)/shard_map/all_gather | solution.py:80
  94.9 66.0 %copy-start.26 = (bf16[1536]{0:T(1024)(128)(2,1)S(1)}, bf16[1536]{0:T(1024)(128)(2,1)}, u32[]{:S(2)}) copy-start(bf16[1536]{0:T(1024)(128)(2,1)} %param.33) | copy-start | bytes 9220
  94.9 66.6 %copy-start.16 = (s32[1,1024]{1,0:T(1,128)S(1)}, s32[1,1024]{1,0:T(1,128)}, u32[]{:S(2)}) copy-start(s32[1,1024]{1,0:T(1,128)} %param.24) | copy-start | bytes 12292
  94.9 403.5 %all-gather.29.cloned.1.call-start = ((), (), s32[]{:S(2)}) async-start(), calls=%async_computation.20 | async-start | bytes 15728640 | tf_op jit(solution)/shard_map/all_gather | solution.py:81
  95.6 486.4 %all-gather.31.cloned.1.call-start = ((), (), s32[]{:S(2)}) async-start(), calls=%async_computation.21 | async-start | bytes 15728640 | tf_op jit(solution)/shard_map/all_gather | solution.py:82
  96.2 766.4 %reduce-scatter.13.cloned.1.call-start = ((), (), s32[]{:S(2)}) async-start(), calls=%async_computation.22 | async-start | bytes 7077888 | tf_op jit(solution)/shard_map/reduce_scatter | solution.py:265
  101.6 0.6 copy-start.18
  402.0 7.5 copy-start.4
  409.5 3.4 copy-start.20
  422.5 159.6 %copy-start.14 = (bf16[1,128,1536]{2,1,0:T(8,128)(2,1)S(1)}, bf16[1,128,1536]{2,1,0:T(8,128)(2,1)}, u32[]{:S(2)}) copy-start(bf16[1,128,1536]{2,1,0:T(8,128)(2,1)} %param.37) | copy-start | bytes 1179652
  593.8 10.2 copy-start
  612.8 9.7 copy-start.2
  622.6 3.5 copy-start.21
  622.6 3.5 copy-start.22
  744.1 0.6 copy-start.17
  744.2 1.4 copy-start.6
  744.2 240.0 %reduce-scatter.15.cloned.1.call-start = ((), (), s32[]{:S(2)}) async-start(), calls=%async_computation.23 | async-start | bytes 7077888 | tf_op jit(solution)/shard_map/reduce_scatter | solution.py:266
  744.8 300.4 %reduce-scatter.17.cloned.1.call-start = ((), (), s32[]{:S(2)}) async-start(), calls=%async_computation.24 | async-start | bytes 110592 | tf_op jit(solution)/shard_map/reduce_scatter | solution.py:267
  745.5 379.6 %reduce-scatter.19.cloned.1.call-start = ((), (), s32[]{:S(2)}) async-start(), calls=%async_computation.25 | async-start | bytes 11796480 | tf_op jit(solution)/shard_map/reduce_scatter | solution.py:290
  750.8 455.3 %reduce-scatter.27.cloned.1.call-start = ((), (), s32[]{:S(2)}) async-start(), calls=%async_computation.29 | async-start | bytes 11796480 | tf_op jit(solution)/shard_map/reduce_scatter | solution.py:302
  755.8 1.1 copy-start.3
  755.9 531.1 %reduce-scatter.29.cloned.1.call-start = ((), (), s32[]{:S(2)}) async-start(), calls=%async_computation.30 | async-start | bytes 11796480 | tf_op jit(solution)/shard_map/reduce_scatter | solution.py:305
  762.9 604.9 %reduce-scatter.21.cloned.1.call-start = ((), (), s32[]{:S(2)}) async-start(), calls=%async_computation.26 | async-start | bytes 11796480 | tf_op jit(solution)/shard_map/reduce_scatter | solution.py:293
  868.9 579.9 %reduce-scatter.23.cloned.1.call-start = ((), (), s32[]{:S(2)}) async-start(), calls=%async_computation.27 | async-start | bytes 11796480 | tf_op jit(solution)/shard_map/reduce_scatter | solution.py:296
  990.4 641.4 %reduce-scatter.31.cloned.1.call-start = ((), (), s32[]{:S(2)}) async-start(), calls=%async_computation.31 | async-start | bytes 31457280 | tf_op jit(solution)/shard_map/reduce_scatter | solution.py:192
  1001.8 813.1 %reduce-scatter.33.cloned.1.call-start = ((), (), s32[]{:S(2)}) async-start(), calls=%async_computation.32 | async-start | bytes 31457280 | tf_op jit(solution)/shard_map/reduce_scatter | solution.py:195
  1013.2 1.0 copy-start.15
  1013.3 984.7 %reduce-scatter.35.cloned.1.call-start = ((), (), s32[]{:S(2)}) async-start(), calls=%async_computation.33 | async-start | bytes 31457280 | tf_op jit(solution)/shard_map/reduce_scatter | solution.py:198
  1025.7 40.8 %copy-start.25 = (f32[128,24]{0,1:T(8,128)S(1)}, f32[128,24]{0,1:T(8,128)}, u32[]{:S(2)}) copy-start(f32[128,24]{0,1:T(8,128)} %get-tuple-element.728) | copy-start | bytes 36868
  1025.8 995.0 %reduce-scatter.25.cloned.1.call-start = ((), (), s32[]{:S(2)}) async-start(), calls=%async_computation.28 | async-start | bytes 184320 | tf_op jit(solution)/shard_map/reduce_scatter | solution.py:299
  1067.7 1869.4 %all-reduce.6.cloned.1.call-start = ((), (), s32[]{:S(2)}) async-start(), calls=%async_computation.34 | async-start | bytes 61341696 | tf_op jit(solution)/shard_map/psum | solution.py:309
  1998.0 9.8 copy-start.5
  2007.8 53.7 %copy-start.7 = (f32[128,1536]{0,1:T(8,128)S(1)}, f32[128,1536]{0,1:T(8,128)}, u32[]{:S(2)}) copy-start(f32[128,1536]{0,1:T(8,128)} %reduce-scatter.13.cloned.1.call-done) | copy-start | bytes 2359300
  2015.1 50.7 %copy-start.8 = (f32[128,1536]{0,1:T(8,128)S(1)}, f32[128,1536]{0,1:T(8,128)}, u32[]{:S(2)}) copy-start(f32[128,1536]{0,1:T(8,128)} %reduce-scatter.15.cloned.1.call-done) | copy-start | bytes 2359300
  2065.8 4.2 copy-start.9
  2065.8 4.2 copy-start.19
  2065.8 4.7 copy-start.23
  2937.1 3.4 copy-start.13
  2937.1 4.8 copy-start.12
  2940.5 2.9 copy-start.11
  2941.9 3.4 copy-start.10
  2941.9 5.7 slice-start.4
  2943.3 4.8 slice-start.5
  2945.3 6.1 slice-start.2
  2948.2 3.7 slice-start.3
  2948.2 6.9 slice-start
  2951.8 4.5 slice-start.1
Sparse Core Ops, SparseCore 0:
  9.6 40.1 all-gather.12
  51.3 37.4 all-gather.18
  90.4 37.4 all-gather.16
  130.5 62.1 all-gather.14
  195.3 59.0 all-gather.20
  255.9 36.0 all-gather.22
  293.5 37.4 all-gather.24
  332.6 82.1 all-gather.26
  416.3 82.0 all-gather.28
  499.9 82.1 all-gather.30
  744.3 118.2 reduce-scatter.12
  866.6 117.4 reduce-scatter.14
  988.0 57.1 reduce-scatter.16
  1047.6 77.4 reduce-scatter.18
  1127.6 78.4 reduce-scatter.26
  1208.5 78.4 reduce-scatter.28
  1289.4 78.4 reduce-scatter.20
  1370.3 78.4 reduce-scatter.22
  1451.3 180.4 reduce-scatter.30
  1634.4 180.4 reduce-scatter.32
  1817.5 180.4 reduce-scatter.34
  2001.1 19.6 reduce-scatter.24
  2027.5 909.4 all-reduce.5
where the time goes:
time: 2980 us; the launch traced here: 2970 us
  waiting for transfers between devices  2310 us (78%)
  matrix products  216 us (7%)
  local copies, waits for them, and re-layouts  208 us (7%)
  blocking collectives  162 us (5%)
  other arithmetic  34.6 us (1%)
    psum x1, waiting for transfers between devices, shards(): lax.psum((ffn_parts[0], ffn_parts[1], ffn_parts[2], attn_parts[0], attn_p...  823 us
    reduce_scatter x1, waiting for transfers between devices, shards(): lax.psum_scatter(weight_grad(normed_two, grad_up_low), 'fsdp', scatter_di...  183 us
    reduce_scatter x1, waiting for transfers between devices, shards(): lax.psum_scatter(weight_grad(hidden, grad_out_low), 'fsdp', scatter_dimen...  183 us
    reduce_scatter x1, waiting for transfers between devices, shards(): lax.psum_scatter(weight_grad(normed_two, grad_gate_low), 'fsdp', scatter_...  183 us
    reduce_scatter x1, waiting for transfers between devices, shards(): lax.psum_scatter(grad_values, 'ctx', scatter_dimension=0, tiled=True)  115 us
    reduce_scatter x1, waiting for transfers between devices, shards(): lax.psum_scatter(grad_keys, 'ctx', scatter_dimension=0, tiled=True)  99.6 us
    reduce_scatter x1, waiting for transfers between devices, shards(): lax.psum_scatter(weight_grad(gated_out, grad_branch_low), 'fsdp', scatter...  80.9 us
    reduce_scatter x1, waiting for transfers between devices, shards(): lax.psum_scatter(weight_grad(normed, grad_value_low), 'fsdp', scatter_dim...  80.9 us
  transfers between devices with their start and end apart: 23, of which 20 were waited for; matrix products, arithmetic and copies ran while one was open for 9% of the time, Pallas kernels for 0%

commit v1 on v0

--- a/solution.py
+++ b/solution.py
@@ -6,6 +6,28 @@
 
 EPSILON = 1e-06
 NEGATIVE = -1e30
+
+
+def joined_along(blocks, dim):
+    blocks = jnp.moveaxis(blocks, 0, dim)
+    shape = blocks.shape
+    return blocks.reshape(*shape[:dim], shape[dim] * shape[dim + 1], *shape[dim + 2 :])
+
+
+def gather_around(x, axis, dim):
+    peers = lax.axis_size(axis)
+    pairs = [(i, (i + 1) % peers) for i in range(peers)]
+    back = [(b, a) for a, b in pairs]
+    lower, upper = ([], [])
+    for step in range(peers - 1):
+        if step % 2 == 0:
+            lower.append(lax.ppermute(lower[-1] if lower else x, axis, pairs))
+        else:
+            upper.append(lax.ppermute(upper[-1] if upper else x, axis, back))
+    blocks = jnp.stack([*lower[::-1], x, *upper])
+    shift = lax.axis_index(axis) - len(lower)
+    blocks = blocks[(jnp.arange(peers) - shift) % peers]
+    return joined_along(blocks, dim)
 
 
 def entering(value, axis, join, neutral, backward):
@@ -78,7 +100,7 @@
         lax.all_gather(w_outgate, "fsdp", axis=0, tiled=True),
         lax.all_gather(w_out, "fsdp", axis=0, tiled=True),
         lax.all_gather(w_gate, "fsdp", axis=0, tiled=True),
-        lax.all_gather(w_up, "fsdp", axis=0, tiled=True),
+        gather_around(w_up, "fsdp", 0),
         lax.all_gather(w_down, "fsdp", axis=0, tiled=True),
     )
     (

time: 2980 us -> 2920 us (0.980)
  waiting for transfers between devices: 2310 us -> 2160 us
  blocking collectives: 162 us -> 196 us
    ppermute x0 -> x3, waiting for transfers between devices: none -> 93.5 us  [the longest x2 93.5 us: gather_around(): lower.append(lax.ppermute(lower[-1] if lower else x, axis, pairs))]
    all_gather x1 -> x0, waiting for transfers between devices: 76 us -> none  [shards(): lax.all_gather(w_up, 'fsdp', axis=0, tiled=True)]
    all_gather x1, waiting for transfers between devices: 75.9 us -> 0.01 us  [shards(): lax.all_gather(w_down, 'fsdp', axis=0, tiled=True)]
    all_gather x1, waiting for transfers between devices: 58.5 us -> 0.02 us  [shards(): lax.all_gather(key_own, 'ctx', axis=0, tiled=True)]
    all_gather x1, blocking collectives: 5.3 us -> 37.9 us  [shards(): lax.all_gather(w_forget, 'fsdp', axis=0, tiled=True)]
  transfers between devices with their start and end apart: 23 -> 25, of which waited for: 20 -> 16; matrix products, arithmetic and copies ran while one was open for 9% -> 11% of each run, Pallas kernels for 0% -> 0%
where the time goes in v1:
time: 2920 us; the launch traced here: 2910 us
  waiting for transfers between devices  2160 us (74%)
  local copies, waits for them, and re-layouts  234 us (8%)
  matrix products  213 us (7%)
  blocking collectives  196 us (7%)
  other arithmetic  64.1 us (2%)
    psum x1, waiting for transfers between devices, shards(): lax.psum((ffn_parts[0], ffn_parts[1], ffn_parts[2], attn_parts[0], attn_p...  823 us
    reduce_scatter x1, waiting for transfers between devices, shards(): lax.psum_scatter(weight_grad(normed_two, grad_up_low), 'fsdp', scatter_di...  183 us
    reduce_scatter x1, waiting for transfers between devices, shards(): lax.psum_scatter(weight_grad(normed_two, grad_gate_low), 'fsdp', scatter_...  183 us
    reduce_scatter x1, waiting for transfers between devices, shards(): lax.psum_scatter(weight_grad(hidden, grad_out_low), 'fsdp', scatter_dimen...  183 us
    reduce_scatter x1, waiting for transfers between devices, shards(): lax.psum_scatter(grad_values, 'ctx', scatter_dimension=0, tiled=True)  115 us
    reduce_scatter x1, waiting for transfers between devices, shards(): lax.psum_scatter(grad_keys, 'ctx', scatter_dimension=0, tiled=True)  97.1 us
    ppermute x2, waiting for transfers between devices, gather_around(): lower.append(lax.ppermute(lower[-1] if lower else x, axis, pairs))  93.5 us
    reduce_scatter x1, waiting for transfers between devices, shards(): lax.psum_scatter(weight_grad(normed, grad_key_low), 'fsdp', scatter_dimen...  80.8 us
  transfers between devices with their start and end apart: 25, of which 16 were waited for; matrix products, arithmetic and copies ran while one was open for 11% of the time, Pallas kernels for 0%

profile of v1, /device:TPU:0, one launch (start us, length us, event | category | flops | bytes accessed | tf_op | source)
XLA Modules:
  0.0 2905.3 jit_solution(17461927499365163301)
XLA Ops:
  11.3 38.5 %all-gather.12.cloned.1.call-done = bf16[1536,1536]{1,0:T(8,128)(2,1)} async-done(((bf16[384,1536]{1,0:T(8,128)(2,1)}), bf16[1536,1536]{1,0:T(8,128)(2,1)}) %all-gather.12.cloned.1.call-update) | async-done | bytes 4718608 | tf_op jit(solution)/shard_map/all_gather | solution.py:98
  49.8 4.0 convolution_convert_fusion.2
  53.9 34.9 %all-gather.18.cloned.1.call-done = bf16[1536,1536]{1,0:T(8,128)(2,1)} async-done(((bf16[384,1536]{1,0:T(8,128)(2,1)}), bf16[1536,1536]{1,0:T(8,128)(2,1)}) %all-gather.18.cloned.1.call-update) | async-done | bytes 4718608 | tf_op jit(solution)/shard_map/all_gather | solution.py:97
  88.8 3.9 convolution_convert_fusion
  96.7 93.5 %collective-permute-done = bf16[384,4096]{1,0:T(8,128)(2,1)} collective-permute-done((bf16[384,4096]{1,0:T(8,128)(2,1)S(1)}, bf16[384,4096]{1,0:T(8,128)(2,1)}, u32[]{:S(2)}, u32[]{:S(2)}) %collective-permute-start) | collective-permute-done | bytes 3145760 | tf_op jit(solution)/shard_map/ppermute | solution.py:24
  190.3 37.9 %all_gather.48 = bf16[1536,24]{0,1:T(8,128)(2,1)S(1)} all-gather(bf16[384,24]{0,1:T(8,128)(2,1)} %param.29), channel_id=1, replica_groups=mesh['ctx'=8,'fsdp'=4] {'fsdp'}, dimensions={0}, use_global_device_ids=true | all-gather | bytes 92160 | tf_op jit(solution)/shard_map/all_gather | solution.py:99
  228.8 2.2 fusion.61
  236.2 22.2 all-reduce
  261.4 8.5 while.65
  272.9 33.7 %all_gather.50 = f32[1024,24]{1,0:T(8,128)} all-gather(f32[128,24]{1,0:T(8,128)} %broadcast_add_fusion), channel_id=1, replica_groups=mesh['ctx'=8,'fsdp'=4] {'ctx'}, dimensions={0}, use_global_device_ids=true | all-gather | bytes 110592 | tf_op jit(solution)/shard_map/all_gather | solution.py:147
  311.4 5.6 pad_maximum_fusion
  317.1 5.1 fusion.78
  322.2 7.0 gather_fusion.1
  329.2 6.6 gather_fusion
  335.8 10.6 pad_maximum_fusion.1
  346.4 3.2 convolution_convert_fusion.1
  350.5 3.2 copy.45
  353.7 4.6 copy.47
  358.9 142.4 %while.63 = (s32[]{:T(128)}, f32[12,128,128]{1,2,0:T(8,128)}, f32[12,2,128]{2,1,0:T(2,128)}, s32[12]{0:T(128)}, bf16[1024,1536]{0,1:T(8,128)(2,1)S(1)}, /*index=...) while((s32[]{:T(128)}, f32[12,128,128]{1,2,0:T(8,128)}, ...), condition=%wide.region_8.9_spmd.clone, body=%wide.region_5.8_spmd.clone.sunk | while | flops 70123272 | bytes 5316909 | solution.py:188
  501.3 2.9 copy.50
  504.1 4.5 multiply_convert_fusion.6
  508.6 3.4 multiply_reduce_fusion.3
  512.2 7.8 fusion.81
  520.0 7.9 fusion.80
  527.9 11.0 multiply_convert_fusion.1
  538.9 9.6 fusion.82
  548.6 9.9 multiply_reduce_fusion.1
  558.8 2.4 multiply_convert_fusion.4
  562.1 3.5 broadcast.170
  565.6 3.5 broadcast.170.clone
  569.1 117.9 %while.64 = (s32[]{:T(128)}, bf16[128,1536]{0,1:T(8,128)(2,1)}, f32[1024,1536]{0,1:T(8,128)}, f32[1024,1536]{0,1:T(8,128)}, f32[128,24]{0,1:T(8,128)S(1)}, /*ind...) while((s32[]{:T(128)}, bf16[128,1536]{0,1:T(8,128)(2,1)}, ...), condition=%wide.region_15.16_spmd.clone, body=%wide.region_11.15_spmd.clone.sunk | while | flops 171998720 | bytes 13599061 | solution.py:283
  688.4 5.2 fusion.52
  693.7 5.0 fusion.64
  699.9 4.9 fusion.56
  705.0 97.1 %reduce-scatter.13.cloned.1.call-done = f32[128,1536]{0,1:T(8,128)} async-done(((f32[1024,1536]{0,1:T(8,128)}), f32[128,1536]{0,1:T(8,128)}) %reduce-scatter.13.cloned.1.call-update) | async-done | bytes 786448 | tf_op jit(solution)/shard_map/reduce_scatter | solution.py:287
  802.1 6.2 fusion.49
  808.6 115.2 %reduce-scatter.15.cloned.1.call-done = f32[128,1536]{0,1:T(8,128)} async-done(((f32[1024,1536]{0,1:T(8,128)}), f32[128,1536]{0,1:T(8,128)}) %reduce-scatter.15.cloned.1.call-update) | async-done | bytes 786448 | tf_op jit(solution)/shard_map/reduce_scatter | solution.py:288
  923.8 6.2 fusion.46
  930.1 11.4 fusion.84
  941.5 11.4 fusion.85
  954.2 10.2 fusion.42
  964.5 20.2 reduce-scatter.17.cloned.1.call-done
  986.2 19.5 all-reduce.1
  1007.7 57.0 %reduce-scatter.19.cloned.1.call-done = f32[384,1536]{1,0:T(8,128)} async-done(((f32[1536,1536]{1,0:T(8,128)}), f32[384,1536]{1,0:T(8,128)}) %reduce-scatter.19.cloned.1.call-update) | async-done | bytes 2359312 | tf_op jit(solution)/shard_map/reduce_scatter | solution.py:312
  1064.8 80.8 %reduce-scatter.27.cloned.1.call-done = f32[384,1536]{1,0:T(8,128)} async-done(((f32[1536,1536]{1,0:T(8,128)}), f32[384,1536]{1,0:T(8,128)}) %reduce-scatter.27.cloned.1.call-update) | async-done | bytes 2359312 | tf_op jit(solution)/shard_map/reduce_scatter | solution.py:324
  1145.6 80.8 %reduce-scatter.29.cloned.1.call-done = f32[384,1536]{1,0:T(8,128)} async-done(((f32[1536,1536]{1,0:T(8,128)}), f32[384,1536]{1,0:T(8,128)}) %reduce-scatter.29.cloned.1.call-update) | async-done | bytes 2359312 | tf_op jit(solution)/shard_map/reduce_scatter | solution.py:327
  1226.4 80.8 %reduce-scatter.21.cloned.1.call-done = f32[384,1536]{1,0:T(8,128)} async-done(((f32[1536,1536]{1,0:T(8,128)}), f32[384,1536]{1,0:T(8,128)}) %reduce-scatter.21.cloned.1.call-update) | async-done | bytes 2359312 | tf_op jit(solution)/shard_map/reduce_scatter | solution.py:315
  1307.2 80.8 %reduce-scatter.23.cloned.1.call-done = f32[384,1536]{1,0:T(8,128)} async-done(((f32[1536,1536]{1,0:T(8,128)}), f32[384,1536]{1,0:T(8,128)}) %reduce-scatter.23.cloned.1.call-update) | async-done | bytes 2359312 | tf_op jit(solution)/shard_map/reduce_scatter | solution.py:318
  1388.1 182.9 %reduce-scatter.31.cloned.1.call-done = f32[384,4096]{1,0:T(8,128)} async-done(((f32[1536,4096]{1,0:T(8,128)}), f32[384,4096]{1,0:T(8,128)}) %reduce-scatter.31.cloned.1.call-update) | async-done | bytes 6291472 | tf_op jit(solution)/shard_map/reduce_scatter | solution.py:214
  1571.0 183.2 %reduce-scatter.33.cloned.1.call-done = f32[384,4096]{1,0:T(8,128)} async-done(((f32[1536,4096]{1,0:T(8,128)}), f32[384,4096]{1,0:T(8,128)}) %reduce-scatter.33.cloned.1.call-update) | async-done | bytes 6291472 | tf_op jit(solution)/shard_map/reduce_scatter | solution.py:217
  1754.2 182.9 %reduce-scatter.35.cloned.1.call-done = f32[1024,1536]{1,0:T(8,128)} async-done(((f32[4096,1536]{1,0:T(8,128)}), f32[1024,1536]{1,0:T(8,128)}) %reduce-scatter.35.cloned.1.call-update) | async-done | bytes 6291472 | tf_op jit(solution)/shard_map/reduce_scatter | solution.py:220
  1938.1 4.9 fusion.83
  1943.0 4.9 fusion.86
  1947.9 7.1 fusion.26
  1955.1 4.9 reduce-scatter.25.cloned.1.call-done
  1960.0 40.7 %psum.88 = f32[384,24]{0,1:T(8,128)} all-reduce(f32[384,24]{0,1:T(8,128)} %reduce-scatter.25.cloned.1.call-done), channel_id=1, replica_groups=mesh['ctx'=8,'fsdp'=4] {'ctx'}, use_global_device_ids=true, to_apply=%region_33.34 | all-reduce | flops 9216 | bytes 73728 | tf_op jit(solution)/shard_map/psum | solution.py:331
  2000.6 4.5 convolution_add_fusion.2
  2005.3 4.1 convolution_add_fusion.1
  2009.9 42.6 %all-reduce.2 = (f32[1536]{0:T(1024)}, f32[24]{0:T(128)}, f32[1536]{0:T(1024)}) all-reduce(f32[1536]{0:T(1024)S(1)} %get-tuple-element.623, f32[24]{0:T(128)S(1)} %copy-done.36, f32[1536]{0:T(1024)S(1)} %copy-done.32), channel_id=1, replica_groups=mesh['ctx'=8,'fsdp'=4] {'ctx','fsdp'}, use_global_device_ids=true, to_apply=%region_25.26 | all-reduce | flops 3096 | bytes 24768 | tf_op jit(solution)/shard_map/psum | solution.py:345
  2053.7 822.6 %all-reduce.6.cloned.1.call-done = (f32[384,1536]{1,0:T(8,128)}, f32[384,1536]{1,0:T(8,128)}, f32[384,1536]{1,0:T(8,128)}, f32[384,1536]{1,0:T(8,128)}, f32[384,...) async-done(((f32[384,1536]{1,0:T(8,128)}, f32[384,1536]{1,0:T(8,128)}, f32[384,1536]{1,0:T(8,128)}, f32[384,1536]{1,0:T(8,128)}, ...) | async-done | bytes 30670864 | tf_op jit(solution)/shard_map/psum | solution.py:331
  2876.3 3.4 copy.121
  2887.3 3.2 copy.126
  2891.0 3.2 copy.127
  2895.5 2.7 copy.128
  (574 shorter events, 298.5 us)
Async XLA Ops:
  7.2 81.7 %copy-start = (bf16[1,128,1536]{2,1,0:T(8,128)(2,1)S(1)}, bf16[1,128,1536]{2,1,0:T(8,128)(2,1)}, u32[]{:S(2)}) copy-start(bf16[1,128,1536]{2,1,0:T(8,128)(2,1)} %param.23) | copy-start | bytes 1179652
  7.2 42.6 %all-gather.12.cloned.1.call-start = ((), (), s32[]{:S(2)}) async-start(), calls=%async_computation.12 | async-start | bytes 5898240 | tf_op jit(solution)/shard_map/all_gather | solution.py:98
  7.9 80.9 %all-gather.18.cloned.1.call-start = ((), (), s32[]{:S(2)}) async-start(), calls=%async_computation.15 | async-start | bytes 5898240 | tf_op jit(solution)/shard_map/all_gather | solution.py:97
  8.7 337.7 %all-gather.16.cloned.1.call-start = ((), (), s32[]{:S(2)}) async-start(), calls=%async_computation.14 | async-start | bytes 5898240 | tf_op jit(solution)/shard_map/all_gather | solution.py:96
  9.4 341.1 %all-gather.14.cloned.1.call-start = ((), (), s32[]{:S(2)}) async-start(), calls=%async_computation.13 | async-start | bytes 3538944 | tf_op jit(solution)/shard_map/all_gather | solution.py:150
  53.9 41.1 %copy-start.12 = (bf16[384,4096]{1,0:T(8,128)(2,1)S(1)}, bf16[384,4096]{1,0:T(8,128)(2,1)}, u32[]{:S(2)}) copy-start(bf16[384,4096]{1,0:T(8,128)(2,1)} %param.35) | copy-start | bytes 9437188
  53.9 299.9 %all-gather.20.cloned.1.call-start = ((), (), s32[]{:S(2)}) async-start(), calls=%async_computation.16 | async-start | bytes 3538944 | tf_op jit(solution)/shard_map/all_gather | solution.py:149
  92.8 411.3 %all-gather.22.cloned.1.call-start = ((), (), s32[]{:S(2)}) async-start(), calls=%async_computation.17 | async-start | bytes 5898240 | tf_op jit(solution)/shard_map/all_gather | solution.py:100
  93.4 415.3 %all-gather.24.cloned.1.call-start = ((), (), s32[]{:S(2)}) async-start(), calls=%async_computation.18 | async-start | bytes 5898240 | tf_op jit(solution)/shard_map/all_gather | solution.py:101
  94.1 216.1 %copy-start.23 = (s32[1,1024]{1,0:T(1,128)S(1)}, s32[1,1024]{1,0:T(1,128)}, u32[]{:S(2)}) copy-start(s32[1,1024]{1,0:T(1,128)} %param.24) | copy-start | bytes 12292
  94.1 425.9 %all-gather.26.cloned.1.call-start = ((), (), s32[]{:S(2)}) async-start(), calls=%async_computation.19 | async-start | bytes 15728640 | tf_op jit(solution)/shard_map/all_gather | solution.py:102
  94.9 433.0 %all-gather.28.cloned.1.call-start = ((), (), s32[]{:S(2)}) async-start(), calls=%async_computation.20 | async-start | bytes 15728640 | tf_op jit(solution)/shard_map/all_gather | solution.py:104
  94.9 95.3 %collective-permute-start = (bf16[384,4096]{1,0:T(8,128)(2,1)S(1)}, bf16[384,4096]{1,0:T(8,128)(2,1)}, u32[]{:S(2)}, u32[]{:S(2)}) collective-permute-start(bf16[384,4096]{1,0:T(8,128)(2,1)S(1)} %copy-done.12), channel_id=1, source_target_pairs={{0,1},{1,2},{2,3},{3,0},{4,5},{5,6},{6,7},{7,4},{8,9},{9,10},{10,1... | collective-permute-start | bytes 9437192 | tf_op jit(solution)/shard_map/ppermute | solution.py:24
  95.2 216.2 %collective-permute-start.2 = (bf16[384,4096]{1,0:T(8,128)(2,1)S(1)}, bf16[384,4096]{1,0:T(8,128)(2,1)}, u32[]{:S(2)}, u32[]{:S(2)}) collective-permute-start(bf16[384,4096]{1,0:T(8,128)(2,1)S(1)} %copy-done.12), channel_id=1, source_target_pairs={{1,0},{2,1},{3,2},{0,3},{5,4},{6,5},{7,6},{4,7},{9,8},{10,9},{11,1... | collective-permute-start | bytes 9437192 | tf_op jit(solution)/shard_map/ppermute | solution.py:26
  190.2 121.2 %collective-permute-start.1 = (bf16[384,4096]{1,0:T(8,128)(2,1)}, bf16[384,4096]{1,0:T(8,128)(2,1)}, u32[]{:S(2)}, u32[]{:S(2)}) collective-permute-start(bf16[384,4096]{1,0:T(8,128)(2,1)} %collective-permute-done), channel_id=1, source_target_pairs={{0,1},{1,2},{2,3},{3,0},{4,5},{5,6},{6,7},{7,4},{8,9},{9,10},{10,1... | collective-permute-start | bytes 9437192 | tf_op jit(solution)/shard_map/ppermute | solution.py:24
  190.2 611.9 %reduce-scatter.13.cloned.1.call-start = ((), (), s32[]{:S(2)}) async-start(), calls=%async_computation.21 | async-start | bytes 7077888 | tf_op jit(solution)/shard_map/reduce_scatter | solution.py:287
  501.2 7.4 copy-start.3
  508.6 3.4 copy-start.27
  520.0 7.9 copy-start.20
  538.9 9.6 copy-start.6
  538.9 9.6 copy-start.5
  548.5 10.2 slice-start
  548.5 10.2 slice-start.1
  548.5 10.2 copy-start.14
  548.6 10.2 copy-start.22
  558.7 6.8 copy-start.1
  561.2 132.4 %copy-start.7 = (bf16[128,1536]{1,0:T(8,128)(2,1)}, bf16[128,1536]{1,0:T(8,128)(2,1)S(1)}, u32[]{:S(2)}) copy-start(bf16[128,1536]{1,0:T(8,128)(2,1)S(1)} %get-tuple-element.727) | copy-start | bytes 1179652
  565.6 3.5 copy-start.28
  565.6 3.5 copy-start.29
  687.0 1.4 copy-start.9
  687.0 236.8 %reduce-scatter.15.cloned.1.call-start = ((), (), s32[]{:S(2)}) async-start(), calls=%async_computation.22 | async-start | bytes 7077888 | tf_op jit(solution)/shard_map/reduce_scatter | solution.py:288
  687.8 296.9 %reduce-scatter.17.cloned.1.call-start = ((), (), s32[]{:S(2)}) async-start(), calls=%async_computation.23 | async-start | bytes 110592 | tf_op jit(solution)/shard_map/reduce_scatter | solution.py:289
  688.4 376.4 %reduce-scatter.19.cloned.1.call-start = ((), (), s32[]{:S(2)}) async-start(), calls=%async_computation.24 | async-start | bytes 11796480 | tf_op jit(solution)/shard_map/reduce_scatter | solution.py:312
  693.6 452.0 %reduce-scatter.27.cloned.1.call-start = ((), (), s32[]{:S(2)}) async-start(), calls=%async_computation.28 | async-start | bytes 11796480 | tf_op jit(solution)/shard_map/reduce_scatter | solution.py:324
  698.7 1.2 copy-start.19
  698.7 527.7 %reduce-scatter.29.cloned.1.call-start = ((), (), s32[]{:S(2)}) async-start(), calls=%async_computation.29 | async-start | bytes 11796480 | tf_op jit(solution)/shard_map/reduce_scatter | solution.py:327
  704.9 602.3 %reduce-scatter.21.cloned.1.call-start = ((), (), s32[]{:S(2)}) async-start(), calls=%async_computation.25 | async-start | bytes 11796480 | tf_op jit(solution)/shard_map/reduce_scatter | solution.py:315
  808.3 579.7 %reduce-scatter.23.cloned.1.call-start = ((), (), s32[]{:S(2)}) async-start(), calls=%async_computation.26 | async-start | bytes 11796480 | tf_op jit(solution)/shard_map/reduce_scatter | solution.py:318
  930.0 641.0 %reduce-scatter.31.cloned.1.call-start = ((), (), s32[]{:S(2)}) async-start(), calls=%async_computation.30 | async-start | bytes 31457280 | tf_op jit(solution)/shard_map/reduce_scatter | solution.py:214
  941.5 812.8 %reduce-scatter.33.cloned.1.call-start = ((), (), s32[]{:S(2)}) async-start(), calls=%async_computation.31 | async-start | bytes 31457280 | tf_op jit(solution)/shard_map/reduce_scatter | solution.py:217
  952.9 1.3 copy-start.21
  952.9 984.2 %reduce-scatter.35.cloned.1.call-start = ((), (), s32[]{:S(2)}) async-start(), calls=%async_computation.32 | async-start | bytes 31457280 | tf_op jit(solution)/shard_map/reduce_scatter | solution.py:220
  964.4 20.3 copy-start.31
  964.4 41.6 %copy-start.35 = (f32[128,24]{0,1:T(8,128)S(1)}, f32[128,24]{0,1:T(8,128)}, u32[]{:S(2)}) copy-start(f32[128,24]{0,1:T(8,128)} %get-tuple-element.730) | copy-start | bytes 36868
  964.4 995.5 %reduce-scatter.25.cloned.1.call-start = ((), (), s32[]{:S(2)}) async-start(), calls=%async_computation.27 | async-start | bytes 184320 | tf_op jit(solution)/shard_map/reduce_scatter | solution.py:321
  1006.7 930.4 %copy-start.33 = (bf16[128,24]{0,1:T(8,128)(2,1)}, bf16[128,24]{0,1:T(8,128)(2,1)S(1)}, u32[]{:S(2)}) copy-start(bf16[128,24]{0,1:T(8,128)(2,1)S(1)} %get-tuple-element.710) | copy-start | bytes 18436
  1007.7 1868.6 %all-reduce.6.cloned.1.call-start = ((), (), s32[]{:S(2)}) async-start(), calls=%async_computation.33 | async-start | bytes 61341696 | tf_op jit(solution)/shard_map/psum | solution.py:331
  1938.1 4.9 copy-start.10
  1955.1 50.1 %copy-start.11 = (f32[128,1536]{0,1:T(8,128)S(1)}, f32[128,1536]{0,1:T(8,128)}, u32[]{:S(2)}) copy-start(f32[128,1536]{0,1:T(8,128)} %reduce-scatter.15.cloned.1.call-done) | copy-start | bytes 2359300
  2005.2 4.2 copy-start.13
  2005.2 4.2 copy-start.26
  2005.2 4.2 copy-start.34
  2005.2 4.7 copy-start.32
  2005.2 4.7 copy-start.36
  2876.3 3.4 copy-start.18
  2876.3 4.8 copy-start.17
  2879.6 2.9 copy-start.16
  2881.1 3.4 copy-start.15
  2881.1 5.7 slice-start.6
  2882.5 4.8 slice-start.7
  2884.4 6.1 slice-start.4
  2887.3 3.7 slice-start.5
  2887.3 6.9 slice-start.2
  2891.0 4.5 slice-start.3
  (6 other events, 5.6 us)
Sparse Core Ops, SparseCore 0:
  9.6 40.1 all-gather.11
  51.3 37.4 all-gather.17
  90.4 62.8 all-gather.15
  155.9 60.4 all-gather.13
  219.0 60.3 all-gather.19
  280.8 36.8 all-gather.21
  319.2 37.4 all-gather.23
  358.3 82.1 all-gather.25
  442.0 82.0 all-gather.27
  687.1 114.8 reduce-scatter.12
  806.3 117.5 reduce-scatter.14
  927.5 57.1 reduce-scatter.16
  987.3 77.4 reduce-scatter.18
  1067.2 78.3 reduce-scatter.26
  1148.0 78.3 reduce-scatter.28
  1228.9 78.3 reduce-scatter.20
  1309.7 78.3 reduce-scatter.22
  1390.5 180.4 reduce-scatter.30
  1573.8 180.4 reduce-scatter.32
  1756.7 180.4 reduce-scatter.34
  1940.3 19.6 reduce-scatter.24
  1966.7 909.5 all-reduce.5
